TPU v7x, 128 devices: a whole 4x4x4 slice. The times are simulated.
128 devices in a mesh: gx: 8 (over z, y_lo), gy: 16 (over x, y_hi, core).
Axes of the slice: x: 4, y: 4 (y_hi: 2, y_lo: 2; y = y_hi * 2 + y_lo), z: 4, core: 2. Of those that a mesh axis runs over, the one named last changes fastest.
Arguments:
- positions: float32 [3, 327680], P(None, ('gx', 'gy')), may hold values from 0 to 1
- velocities: float32 [3, 327680], P(None, ('gx', 'gy')), may hold values from -6 to 6
- block_order: int32 [128, 20], P(('gx', 'gy')), may hold values from 0 to 19, each once within a row
- flags: int32 [128, 20], P(('gx', 'gy')), may hold values from 0 to 1, as said below
- offsets: int32 [3, 3], replicated, may hold values from -1 to 1
- pixels: int32 [3, 327680], P(None, ('gx', 'gy')), may hold values from 0 to 1048575, as said below
Outputs:
- new_positions: float32 [3, 327680], P(None, ('gx', 'gy'))
- new_velocities: float32 [3, 327680], P(None, ('gx', 'gy'))
- maps: float32 [8192, 384], P(('gx', 'gy'))
Inputs may be any that keep to these rules, and one draw needn't show every extreme that they name: `flags`: each row holds 1 to 5 ones, and some row holds exactly 5. `block_order`: each row is a permutation. Among the 2560 columns of one slab cell and one replica, every strip of 8192 consecutive pixels is named exactly 2560 / 128 times.
All inputs are finite; a program needn't handle non-finite values.
Results may differ from a plain program's by a relative error of at most 0.0028.
Values may be sent and summed in bfloat16 or wider, within the bound.
A program may use at most 448 MiB of HBM per device.

v0:
```python
import jax
import jax.numpy as jnp
from jax import lax
from jax.sharding import PartitionSpec as P

MOVERS = 2
CROSS_MAX = 5
REPLICAS = 3
STRIP_ROWS = 64
time_step = 0.05
lane_count = 128


def passed_along(block, axis, distance):
    devices = range(lax.axis_size(axis))
    route = [((i - distance) % len(devices), i) for i in devices]
    return lax.ppermute(block, axis, route)


def sky_terms(shifted, speeds, live_mask):
    radius = jnp.sum(shifted * shifted, axis=1)
    weight = 1.0 / (1.0 + radius)
    radial = jnp.sum(speeds[None] * shifted, axis=1) / jnp.sqrt(1.0 + radius)
    energy = jnp.sum(speeds * speeds, axis=0) / 3.0
    return jnp.stack(
        [weight * live_mask, weight * radial * live_mask, weight * energy[None] * live_mask], axis=0
    ).astype(jnp.bfloat16)


def deposit(values, pixel_ids, target_of, row_total):
    entries = values.shape[0] * values.shape[2]
    flat_values = jnp.transpose(values, (0, 2, 1)).reshape(entries, 3)
    flat_ids = pixel_ids.reshape(entries)
    target = target_of(flat_ids // lane_count)
    lane_ids = flat_ids % lane_count
    row_hits = (target[None, :] == jnp.arange(row_total, dtype=jnp.int32)[:, None]).astype(
        jnp.bfloat16
    )
    lane_hits = (lane_ids[:, None] == jnp.arange(lane_count, dtype=jnp.int32)[None, :]).astype(
        jnp.bfloat16
    )
    spread = (flat_values[:, :, None] * lane_hits[:, None, :]).reshape(entries, 3 * lane_count)
    return jnp.dot(row_hits, spread, preferred_element_type=jnp.float32)


def on_device(positions, velocities, block_order, flags, offsets, pixels):
    blocks = block_order.shape[1]
    width = positions.shape[1] // blocks
    places = positions.reshape(3, blocks, width)
    speeds = velocities.reshape(3, blocks, width)
    places = places + time_step * speeds
    ordering = block_order[0]
    places = jnp.take(places, ordering, axis=1)
    speeds = jnp.take(speeds, ordering, axis=1)

    def leaving(which_set, component, sign_step):
        first_block = which_set * MOVERS
        moved_pos = places[:, first_block : first_block + MOVERS].at[component].add(sign_step)
        return (moved_pos, speeds[:, first_block : first_block + MOVERS])

    east_pos, east_vel = leaving(0, 0, -1.0)
    from_west = passed_along((east_pos, east_vel), "gx", 1)
    west_pos, west_vel = leaving(1, 0, 1.0)
    from_east = passed_along((west_pos, west_vel), "gx", -1)
    north_pos, north_vel = leaving(2, 1, -1.0)
    from_south = passed_along((north_pos, north_vel), "gy", 1)
    south_pos, south_vel = leaving(3, 1, 1.0)
    from_north = passed_along((south_pos, south_vel), "gy", -1)
    arrived = (from_west, from_east, from_south, from_north)
    new_places = jnp.concatenate(
        [places[:, 4 * MOVERS :]] + [received[0] for received in arrived], axis=1
    )
    new_speeds = jnp.concatenate(
        [speeds[:, 4 * MOVERS :]] + [received[1] for received in arrived], axis=1
    )
    count_x = lax.axis_size("gx")
    count_y = lax.axis_size("gy")
    cell_x = lax.axis_index("gx")
    cell_y = lax.axis_index("gy")
    owner_index = cell_x * count_y + cell_y
    flag_row = flags[0]
    ranking = (1 - flag_row) * blocks + jnp.arange(blocks, dtype=jnp.int32)
    chosen = jnp.argsort(ranking)[:CROSS_MAX]
    live_mask = jnp.take(flag_row, chosen).astype(jnp.float32).reshape(1, CROSS_MAX, 1)
    picked_pos = jnp.take(new_places, chosen, axis=1)
    picked_vel = jnp.take(new_speeds, chosen, axis=1)
    picked_ids = jnp.take(pixels.reshape(REPLICAS, blocks, width), chosen, axis=1)
    global_pos = jnp.stack(
        [
            (cell_x.astype(jnp.float32) + picked_pos[0]) / count_x,
            (cell_y.astype(jnp.float32) + picked_pos[1]) / count_y,
            picked_pos[2],
        ],
        axis=0,
    )
    shifted = global_pos[None] + offsets.astype(jnp.float32)[:, :, None, None]
    values = sky_terms(shifted, picked_vel, live_mask)
    send_values = jnp.transpose(values, (2, 0, 1, 3)).reshape(CROSS_MAX, 3, REPLICAS * width)
    send_ids = jnp.transpose(picked_ids, (1, 0, 2)).reshape(CROSS_MAX, REPLICAS * width)

    def in_strip(rows_global):
        return rows_global - owner_index * STRIP_ROWS

    maps = deposit(
        lax.all_gather(send_values, ("gx", "gy"), axis=0, tiled=True),
        lax.all_gather(send_ids, ("gx", "gy"), axis=0, tiled=True),
        in_strip,
        STRIP_ROWS,
    )
    return (new_places.reshape(3, blocks * width), new_speeds.reshape(3, blocks * width), maps)


def solution(mesh):
    in_specs = (
        P(None, ("gx", "gy")),
        P(None, ("gx", "gy")),
        P(("gx", "gy"), None),
        P(("gx", "gy"), None),
        P(),
        P(None, ("gx", "gy")),
    )
    out_specs = (P(None, ("gx", "gy")), P(None, ("gx", "gy")), P(("gx", "gy"), None))
    return jax.shard_map(
        on_device, mesh=mesh, in_specs=in_specs, out_specs=out_specs, check_vma=False
    )
```

profile of v0, /device:TPU:1, one launch (start us, length us, event | category | flops | bytes accessed | tf_op | source)
XLA Modules:
  0.0 567.8 jit_solution(4110377059390207661)
XLA Ops:
  7.2 0.7 compare_and_fusion
  7.9 0.7 compare_select_fusion
  8.6 0.8 bitcast_add_fusion
  9.4 1.4 gather_fusion.3
  10.7 0.6 gather_fusion.2
  11.3 0.1 select_bitcast_fusion
  11.4 1.5 collective-permute-start.7
  12.9 3.0 collective-permute-start.6
  15.9 4.5 collective-permute-start.5
  20.4 0.9 collective-permute-start.2
  21.4 0.7 iota_add_fusion
  22.1 1.6 sort.17
  23.7 1.3 gather_fusion.1
  25.0 0.6 gather_fusion
  25.6 0.1 broadcast_select_fusion
  25.7 183.7 %all-gather = s32[128,5,384]{2,1,0:T(8,128)S(1)} all-gather(s32[1,5,384]{2,1,0:T(8,128)S(1)} %reshape.342), channel_id=1, replica_groups=mesh['gx'=8,'gy'=16] {'gx','gy'}, dimensions={0}, use_global_device_ids=true | all-gather | bytes 990720 | tf_op jit(solution)/shard_map/all_gather | solution.py:106
  209.4 0.2 reshape.286
  209.6 0.9 fusion.3
  210.4 0.7 convert_element_type.25
  211.3 3.6 collective-permute-start.1
  214.9 0.7 collective-permute-start.3
  215.6 0.6 gather_fusion.5
  216.2 0.1 multiply_reduce_fusion
  216.4 3.0 collective-permute-done.3
  219.4 0.6 gather_fusion.4
  220.0 0.1 select_bitcast_fusion.3
  220.1 0.1 fusion.7
  220.3 0.6 reshape.287
  221.0 20.2 %fusion = bf16[245760,128]{0,1:T(8,128)(2,1)} fusion(s32[245760]{0:T(1024)S(1)} %get-tuple-element.62), kind=kLoop, calls=%fused_computation.7 | loop fusion | flops 62914560 | bytes 63897600 | tf_op jit(solution)/shard_map/convert_element_type | solution.py:39
  241.2 169.5 %all-gather.3.cloned.1.call-done = bf16[640,3,384]{2,1,0:T(4,128)(2,1)} async-done(((bf16[5,3,384]{2,1,0:T(4,128)(2,1)}), bf16[640,3,384]{2,1,0:T(4,128)(2,1)}) %all-gather.3.cloned.1.call-update) | async-done | bytes 1474576 | tf_op jit(solution)/shard_map/all_gather | solution.py:105
  410.7 81.4 %broadcast_multiply_fusion = bf16[245760,3,128]{0,2,1:T(8,128)(2,1)} fusion(bf16[245760,128]{0,1:T(8,128)(2,1)} %fusion, bf16[245760,3]{0,1:T(4,128)(2,1)} %bitcast.48), kind=kLoop, calls=%fused_computation.8 | loop fusion | flops 94371840 | bytes 253132800 | tf_op jit(solution)/shard_map/mul | solution.py:42
  492.2 68.8 %fusion.1 = f32[64,384]{1,0:T(8,128)} fusion(bf16[245760,384]{0,1:T(8,128)(2,1)} %bitcast.16, s32[245760]{0:T(1024)S(1)} %get-tuple-element.61), kind=kOutput, calls=%fused_computation.10 | convolution fusion | flops 12095324160 | bytes 189825024 | tf_op jit(solution)/shard_map/dot_general | solution.py:43
  (48 shorter events, 0.6 us)
Async XLA Ops:
  7.2 17.8 %copy-start = (s32[3,2560]{1,0:T(4,128)S(1)}, s32[3,2560]{1,0:T(4,128)}, u32[]{:S(2)}) copy-start(s32[3,2560]{1,0:T(4,128)} %param.23) | copy-start | bytes 92164
  7.2 403.5 %all-gather.3.cloned.1.call-start = ((), (), s32[]{:S(2)}) async-start(), calls=%async_computation | async-start | bytes 1981440 | tf_op jit(solution)/shard_map/all_gather | solution.py:105
  11.4 204.2 %collective-permute-start.7 = (f32[3,2,128]{2,0,1:T(4,128)S(1)}, f32[3,2,128]{2,0,1:T(4,128)S(1)}, u32[]{:S(2)}, u32[]{:S(2)}) collective-permute-start(f32[3,2,128]{2,0,1:T(4,128)S(1)} %get-tuple-element.63), channel_id=1, source_target_pairs={{1,0},{2,1},{3,2},{4,3},{5,4},{6,5},{7,6},{8,7},{9,8},{10,9},{11,1... | collective-permute-start | bytes 9224 | tf_op jit(solution)/shard_map/ppermute | solution.py:17
  12.9 201.9 %collective-permute-start.6 = (f32[3,2,128]{2,0,1:T(4,128)S(1)}, f32[3,2,128]{2,0,1:T(4,128)S(1)}, u32[]{:S(2)}, u32[]{:S(2)}) collective-permute-start(f32[3,2,128]{2,0,1:T(4,128)S(1)} %get-tuple-element.64), channel_id=1, source_target_pairs={{15,0},{0,1},{1,2},{2,3},{3,4},{4,5},{5,6},{6,7},{7,8},{8,9},{9,10... | collective-permute-start | bytes 9224 | tf_op jit(solution)/shard_map/ppermute | solution.py:17
  15.9 195.4 %collective-permute-start.5 = (f32[3,2,128]{2,0,1:T(4,128)S(1)}, f32[3,2,128]{2,0,1:T(4,128)S(1)}, u32[]{:S(2)}, u32[]{:S(2)}) collective-permute-start(f32[3,2,128]{2,0,1:T(4,128)S(1)} %get-tuple-element.65), channel_id=1, source_target_pairs={{16,0},{32,16},{48,32},{64,48},{80,64},{96,80},{112,96},{0,112},{1... | collective-permute-start | bytes 9224 | tf_op jit(solution)/shard_map/ppermute | solution.py:17
  20.4 190.9 %collective-permute-start.4 = (f32[3,2,128]{2,0,1:T(4,128)S(1)}, f32[3,2,128]{2,0,1:T(4,128)S(1)}, u32[]{:S(2)}, u32[]{:S(2)}) collective-permute-start(f32[3,2,128]{2,0,1:T(4,128)S(1)} %get-tuple-element.66), channel_id=1, source_target_pairs={{112,0},{0,16},{16,32},{32,48},{48,64},{64,80},{80,96},{96,112},{1... | collective-permute-start | bytes 9224 | tf_op jit(solution)/shard_map/ppermute | solution.py:17
  20.4 195.9 %collective-permute-start.2 = (f32[3,2,128]{2,0,1:T(4,128)S(1)}, f32[3,2,128]{2,0,1:T(4,128)S(1)}, u32[]{:S(2)}, u32[]{:S(2)}) collective-permute-start(f32[3,2,128]{2,0,1:T(4,128)S(1)} %scatter-add.16), channel_id=1, source_target_pairs={{15,0},{0,1},{1,2},{2,3},{3,4},{4,5},{5,6},{6,7},{7,8},{8,9},{9,10... | collective-permute-start | bytes 9224 | tf_op jit(solution)/shard_map/ppermute | solution.py:17
  211.2 5.1 collective-permute-start
  211.3 5.0 collective-permute-start.1
  214.9 4.5 collective-permute-start.3
  215.6 276.5 %copy-start.3 = (f32[3,20,128]{2,0,1:T(4,128)}, f32[3,20,128]{2,0,1:T(4,128)S(1)}, u32[]{:S(2)}) copy-start(f32[3,20,128]{2,0,1:T(4,128)S(1)} %constant_dynamic-update-slice_fusion.4) | copy-start | bytes 92164
  219.4 272.7 %copy-start.2 = (f32[3,20,128]{2,0,1:T(4,128)}, f32[3,20,128]{2,0,1:T(4,128)S(1)}, u32[]{:S(2)}) copy-start(f32[3,20,128]{2,0,1:T(4,128)S(1)} %constant_dynamic-update-slice_fusion) | copy-start | bytes 92164
  492.2 68.8 %copy-start.1 = (s32[3,2560]{1,0:T(4,128)S(1)}, s32[3,2560]{1,0:T(4,128)}, u32[]{:S(2)}) copy-start(s32[3,2560]{1,0:T(4,128)} %param.23) | copy-start | bytes 92164
Sparse Core Ops, SparseCore 0:
  221.1 189.5 all-gather.2
where the time goes:
time: 569 us; the launch traced here: 568 us
  blocking collectives  184 us (32%)
  waiting for transfers between devices  173 us (30%)
  other arithmetic  108 us (19%)
  matrix products  68.8 us (12%)
  starting transfers between devices  14.3 us (3%)
  between operations  14.3 us (3%)
  local copies, waits for them, and re-layouts  6.05 us (1%)
    all_gather x1, blocking collectives, on_device(): lax.all_gather(send_ids, ('gx', 'gy'), axis=0, tiled=True)  184 us
    all_gather x1, waiting for transfers between devices, on_device(): lax.all_gather(send_values, ('gx', 'gy'), axis=0, tiled=True)  170 us
    mul x1, other arithmetic, deposit(): flat_values[:, :, None] * lane_hits[:, None, :]  81.4 us
    dot_general x1, matrix products, deposit(): return jnp.dot(row_hits, spread, preferred_element_type=jnp.float32)  68.8 us
    convert_element_type x1, other arithmetic, deposit(): (lane_ids[:, None] == jnp.arange(lane_count, dtype=jnp.int32)[None, :]).a...  20.2 us
    ppermute x8, starting transfers between devices, passed_along(): return lax.ppermute(block, axis, route)  14.2 us
  transfers between devices with their start and end apart: 9, of which 2 were waited for; matrix products, arithmetic and copies ran while one was open for 5% of the time, Pallas kernels for 0%

commit v1 on v0

--- a/solution.py
+++ b/solution.py
@@ -1,3 +1,4 @@
+import functools
 import jax
 import jax.numpy as jnp
 from jax import lax
@@ -9,6 +10,21 @@
 STRIP_ROWS = 64
 time_step = 0.05
 lane_count = 128
+
+
+def sources_all_mark(x_local, mesh_dim):
+    return jnp.concatenate(
+        lax.all_to_all(
+            jnp.stack([x_local] * lax.axis_size(mesh_dim), axis=0),
+            axis_name=mesh_dim,
+            split_axis=0,
+            concat_axis=0,
+        ),
+        0,
+    )
+
+
+match_numbers_now = functools.partial(sources_all_mark, mesh_dim=("gx", "gy"))
 
 
 def passed_along(block, axis, distance):
@@ -103,7 +119,7 @@
 
     maps = deposit(
         lax.all_gather(send_values, ("gx", "gy"), axis=0, tiled=True),
-        lax.all_gather(send_ids, ("gx", "gy"), axis=0, tiled=True),
+        match_numbers_now(send_ids),
         in_strip,
         STRIP_ROWS,
     )

time: 569 us -> 419 us (0.74)
  blocking collectives: 184 us -> 0 us
  starting transfers between devices: 14.3 us -> 35.5 us
  waiting for transfers between devices: 173 us -> 185 us
    all_gather x1 -> x0, blocking collectives: 184 us -> none  [on_device(): lax.all_gather(send_ids, ('gx', 'gy'), axis=0, tiled=True)]
    all_to_all x0 -> x1, starting transfers between devices: none -> 11.7 us  [sources_all_mark(): lax.all_to_all(jnp.stack([x_local] * lax.axis_size(mesh_dim), axis=0), ax...]
    ppermute x8, starting transfers between devices: 14.2 us -> 23.8 us  [passed_along(): return lax.ppermute(block, axis, route)]
    all_gather x1, waiting for transfers between devices: 170 us -> 176 us  [on_device(): lax.all_gather(send_values, ('gx', 'gy'), axis=0, tiled=True)]
  transfers between devices with their start and end apart: 9 -> 10, of which waited for: 2 -> 4; matrix products, arithmetic and copies ran while one was open for 5% -> 7% of each run, Pallas kernels for 0% -> 0%
where the time goes in v1:
time: 419 us
  waiting for transfers between devices  185 us (44%)
  other arithmetic  108 us (26%)
  matrix products  68.8 us (16%)
  starting transfers between devices  35.5 us (8%)
  between operations  14.3 us (3%)
  local copies, waits for them, and re-layouts  7.31 us (2%)
    all_gather x1, waiting for transfers between devices, on_device(): lax.all_gather(send_values, ('gx', 'gy'), axis=0, tiled=True)  176 us
    mul x1, other arithmetic, deposit(): flat_values[:, :, None] * lane_hits[:, None, :]  81.4 us
    dot_general x1, matrix products, deposit(): return jnp.dot(row_hits, spread, preferred_element_type=jnp.float32)  68.8 us
    ppermute x8, starting transfers between devices, passed_along(): return lax.ppermute(block, axis, route)  23.8 us
    convert_element_type x1, other arithmetic, deposit(): (lane_ids[:, None] == jnp.arange(lane_count, dtype=jnp.int32)[None, :]).a...  20.1 us
    all_to_all x1, starting transfers between devices, sources_all_mark(): lax.all_to_all(jnp.stack([x_local] * lax.axis_size(mesh_dim), axis=0), ax...  11.7 us
    ppermute x8, waiting for transfers between devices, passed_along(): return lax.ppermute(block, axis, route)  8.53 us
  transfers between devices with their start and end apart: 10, of which 4 were waited for; matrix products, arithmetic and copies ran while one was open for 7% of the time, Pallas kernels for 0%

profile of v1, /device:TPU:1, one launch (start us, length us, event | category | flops | bytes accessed | tf_op | source)
XLA Modules:
  0.0 418.6 jit_solution(8564426414978760230)
XLA Ops:
  7.2 0.7 compare_and_fusion
  7.9 0.7 compare_select_fusion
  8.5 0.8 bitcast_add_fusion
  9.3 1.4 gather_fusion.3
  10.7 0.6 gather_fusion.2
  11.3 0.1 select_bitcast_fusion
  11.4 1.5 collective-permute-start.7
  12.9 3.0 collective-permute-start.6
  15.9 4.5 %collective-permute-start.5 = (f32[3,2,128]{2,0,1:T(4,128)S(1)}, f32[3,2,128]{2,0,1:T(4,128)S(1)}, u32[]{:S(2)}, u32[]{:S(2)}) collective-permute-start(f32[3,2,128]{2,0,1:T(4,128)S(1)} %get-tuple-element.65), channel_id=1, source_target_pairs={{16,0},{32,16},{48,32},{64,48},{80,64},{96,80},{112,96},{0,112},{1... | collective-permute-start | bytes 9224 | tf_op jit(solution)/shard_map/ppermute | solution.py:33
  20.5 0.7 iota_add_fusion
  21.1 1.6 sort.17
  22.8 0.6 gather_fusion
  23.4 1.3 stack.7
  24.7 11.7 %all-to-all-start = ((s32[128,5,384]{2,1,0:T(8,128)}), s32[128,5,384]{2,1,0:T(8,128)S(1)}, u32[]{:S(2)}, u32[]{:S(2)}) async-start(s32[128,5,384]{2,1,0:T(8,128)} %stack.7), calls=%async_computation | async-start | bytes 3145728 | tf_op jit(solution)/shard_map/all_to_all | solution.py:17
  36.5 1.3 gather_fusion.1
  37.8 0.7 convert_element_type.25
  38.6 4.3 %collective-permute-start.1 = (f32[3,2,128]{2,0,1:T(4,128)S(1)}, f32[3,2,128]{2,0,1:T(4,128)S(1)}, u32[]{:S(2)}, u32[]{:S(2)}) collective-permute-start(f32[3,2,128]{2,0,1:T(4,128)S(1)} %scatter-add.15), channel_id=1, source_target_pairs={{16,0},{32,16},{48,32},{64,48},{80,64},{96,80},{112,96},{0,112},{1... | collective-permute-start | bytes 9224 | tf_op jit(solution)/shard_map/ppermute | solution.py:33
  42.9 7.0 %collective-permute-done.1 = f32[3,2,128]{2,0,1:T(4,128)S(1)} collective-permute-done((f32[3,2,128]{2,0,1:T(4,128)S(1)}, f32[3,2,128]{2,0,1:T(4,128)S(1)}, u32[]{:S(2)}, u32[]{:S(2)}) %collective-permute-start.1) | collective-permute-done | bytes 3104 | tf_op jit(solution)/shard_map/ppermute | solution.py:33
  49.9 4.5 %collective-permute-start.2 = (f32[3,2,128]{2,0,1:T(4,128)S(1)}, f32[3,2,128]{2,0,1:T(4,128)S(1)}, u32[]{:S(2)}, u32[]{:S(2)}) collective-permute-start(f32[3,2,128]{2,0,1:T(4,128)S(1)} %scatter-add.16), channel_id=1, source_target_pairs={{15,0},{0,1},{1,2},{2,3},{3,4},{4,5},{5,6},{6,7},{7,8},{8,9},{9,10... | collective-permute-start | bytes 9224 | tf_op jit(solution)/shard_map/ppermute | solution.py:33
  54.3 0.7 collective-permute-done.2
  55.1 6.0 %collective-permute-start.3 = (f32[3,2,128]{2,0,1:T(4,128)S(1)}, f32[3,2,128]{2,0,1:T(4,128)S(1)}, u32[]{:S(2)}, u32[]{:S(2)}) collective-permute-start(f32[3,2,128]{2,0,1:T(4,128)S(1)} %scatter-add.19), channel_id=1, source_target_pairs={{1,0},{2,1},{3,2},{4,3},{5,4},{6,5},{7,6},{8,7},{9,8},{10,9},{11,1... | collective-permute-start | bytes 9224 | tf_op jit(solution)/shard_map/ppermute | solution.py:33
  61.1 0.8 collective-permute-done.3
  61.9 0.6 gather_fusion.4
  62.7 0.6 gather_fusion.5
  63.4 0.1 fusion.7
  63.6 0.6 reshape.281
  64.2 0.2 reshape_reshape.3
  64.4 0.9 fusion.3
  65.3 20.1 %fusion = bf16[245760,128]{0,1:T(8,128)(2,1)} fusion(s32[245760]{0:T(1024)S(1)} %get-tuple-element.62), kind=kLoop, calls=%fused_computation.7 | loop fusion | flops 62914560 | bytes 63897600 | tf_op jit(solution)/shard_map/convert_element_type | solution.py:55
  85.4 176.0 %all-gather.2.cloned.1.call-done = bf16[640,3,384]{2,1,0:T(4,128)(2,1)} async-done(((bf16[5,3,384]{2,1,0:T(4,128)(2,1)}), bf16[640,3,384]{2,1,0:T(4,128)(2,1)}) %all-gather.2.cloned.1.call-update) | async-done | bytes 1474576 | tf_op jit(solution)/shard_map/all_gather | solution.py:121
  261.4 81.4 %broadcast_multiply_fusion = bf16[245760,3,128]{0,2,1:T(8,128)(2,1)} fusion(bf16[245760,128]{0,1:T(8,128)(2,1)} %fusion, bf16[245760,3]{0,1:T(4,128)(2,1)} %bitcast.53), kind=kLoop, calls=%fused_computation.8 | loop fusion | flops 94371840 | bytes 253132800 | tf_op jit(solution)/shard_map/mul | solution.py:58
  342.9 68.8 %fusion.1 = f32[64,384]{1,0:T(8,128)} fusion(bf16[245760,384]{0,1:T(8,128)(2,1)} %bitcast.16, s32[245760]{0:T(1024)S(1)} %get-tuple-element.61), kind=kOutput, calls=%fused_computation.10 | convolution fusion | flops 12095324160 | bytes 189825024 | tf_op jit(solution)/shard_map/dot_general | solution.py:59
  (49 shorter events, 0.8 us)
Async XLA Ops:
  7.2 15.6 %copy-start = (s32[3,2560]{1,0:T(4,128)S(1)}, s32[3,2560]{1,0:T(4,128)}, u32[]{:S(2)}) copy-start(s32[3,2560]{1,0:T(4,128)} %param.23) | copy-start | bytes 92164
  11.4 51.3 %collective-permute-start.7 = (f32[3,2,128]{2,0,1:T(4,128)S(1)}, f32[3,2,128]{2,0,1:T(4,128)S(1)}, u32[]{:S(2)}, u32[]{:S(2)}) collective-permute-start(f32[3,2,128]{2,0,1:T(4,128)S(1)} %get-tuple-element.63), channel_id=1, source_target_pairs={{1,0},{2,1},{3,2},{4,3},{5,4},{6,5},{7,6},{8,7},{9,8},{10,9},{11,1... | collective-permute-start | bytes 9224 | tf_op jit(solution)/shard_map/ppermute | solution.py:33
  12.9 49.7 %collective-permute-start.6 = (f32[3,2,128]{2,0,1:T(4,128)S(1)}, f32[3,2,128]{2,0,1:T(4,128)S(1)}, u32[]{:S(2)}, u32[]{:S(2)}) collective-permute-start(f32[3,2,128]{2,0,1:T(4,128)S(1)} %get-tuple-element.64), channel_id=1, source_target_pairs={{15,0},{0,1},{1,2},{2,3},{3,4},{4,5},{5,6},{6,7},{7,8},{8,9},{9,10... | collective-permute-start | bytes 9224 | tf_op jit(solution)/shard_map/ppermute | solution.py:33
  15.9 46.7 %collective-permute-start.5 = (f32[3,2,128]{2,0,1:T(4,128)S(1)}, f32[3,2,128]{2,0,1:T(4,128)S(1)}, u32[]{:S(2)}, u32[]{:S(2)}) collective-permute-start(f32[3,2,128]{2,0,1:T(4,128)S(1)} %get-tuple-element.65), channel_id=1, source_target_pairs={{16,0},{32,16},{48,32},{64,48},{80,64},{96,80},{112,96},{0,112},{1... | collective-permute-start | bytes 9224 | tf_op jit(solution)/shard_map/ppermute | solution.py:33
  20.3 42.3 %collective-permute-start.4 = (f32[3,2,128]{2,0,1:T(4,128)S(1)}, f32[3,2,128]{2,0,1:T(4,128)S(1)}, u32[]{:S(2)}, u32[]{:S(2)}) collective-permute-start(f32[3,2,128]{2,0,1:T(4,128)S(1)} %get-tuple-element.66), channel_id=1, source_target_pairs={{112,0},{0,16},{16,32},{32,48},{48,64},{64,80},{80,96},{96,112},{1... | collective-permute-start | bytes 9224 | tf_op jit(solution)/shard_map/ppermute | solution.py:33
  20.4 18.2 %collective-permute-start = (f32[3,2,128]{2,0,1:T(4,128)S(1)}, f32[3,2,128]{2,0,1:T(4,128)S(1)}, u32[]{:S(2)}, u32[]{:S(2)}) collective-permute-start(f32[3,2,128]{2,0,1:T(4,128)S(1)} %scatter-add.14), channel_id=1, source_target_pairs={{112,0},{0,16},{16,32},{32,48},{48,64},{64,80},{80,96},{96,112},{1... | collective-permute-start | bytes 9224 | tf_op jit(solution)/shard_map/ppermute | solution.py:33
  24.7 39.6 %all-to-all-start = ((s32[128,5,384]{2,1,0:T(8,128)}), s32[128,5,384]{2,1,0:T(8,128)S(1)}, u32[]{:S(2)}, u32[]{:S(2)}) async-start(s32[128,5,384]{2,1,0:T(8,128)} %stack.7), calls=%async_computation | async-start | bytes 3145728 | tf_op jit(solution)/shard_map/all_to_all | solution.py:17
  36.4 225.0 %all-gather.2.cloned.1.call-start = ((), (), s32[]{:S(2)}) async-start(), calls=%async_computation.1 | async-start | bytes 1981440 | tf_op jit(solution)/shard_map/all_gather | solution.py:121
  38.6 11.3 %collective-permute-start.1 = (f32[3,2,128]{2,0,1:T(4,128)S(1)}, f32[3,2,128]{2,0,1:T(4,128)S(1)}, u32[]{:S(2)}, u32[]{:S(2)}) collective-permute-start(f32[3,2,128]{2,0,1:T(4,128)S(1)} %scatter-add.15), channel_id=1, source_target_pairs={{16,0},{32,16},{48,32},{64,48},{80,64},{96,80},{112,96},{0,112},{1... | collective-permute-start | bytes 9224 | tf_op jit(solution)/shard_map/ppermute | solution.py:33
  49.9 5.2 %collective-permute-start.2 = (f32[3,2,128]{2,0,1:T(4,128)S(1)}, f32[3,2,128]{2,0,1:T(4,128)S(1)}, u32[]{:S(2)}, u32[]{:S(2)}) collective-permute-start(f32[3,2,128]{2,0,1:T(4,128)S(1)} %scatter-add.16), channel_id=1, source_target_pairs={{15,0},{0,1},{1,2},{2,3},{3,4},{4,5},{5,6},{6,7},{7,8},{8,9},{9,10... | collective-permute-start | bytes 9224 | tf_op jit(solution)/shard_map/ppermute | solution.py:33
  55.1 6.8 %collective-permute-start.3 = (f32[3,2,128]{2,0,1:T(4,128)S(1)}, f32[3,2,128]{2,0,1:T(4,128)S(1)}, u32[]{:S(2)}, u32[]{:S(2)}) collective-permute-start(f32[3,2,128]{2,0,1:T(4,128)S(1)} %scatter-add.19), channel_id=1, source_target_pairs={{1,0},{2,1},{3,2},{4,3},{5,4},{6,5},{7,6},{8,7},{9,8},{10,9},{11,1... | collective-permute-start | bytes 9224 | tf_op jit(solution)/shard_map/ppermute | solution.py:33
  61.9 280.9 %copy-start.3 = (f32[3,20,128]{2,0,1:T(4,128)}, f32[3,20,128]{2,0,1:T(4,128)S(1)}, u32[]{:S(2)}) copy-start(f32[3,20,128]{2,0,1:T(4,128)S(1)} %constant_dynamic-update-slice_fusion) | copy-start | bytes 92164
  62.7 280.2 %copy-start.2 = (f32[3,20,128]{2,0,1:T(4,128)}, f32[3,20,128]{2,0,1:T(4,128)S(1)}, u32[]{:S(2)}) copy-start(f32[3,20,128]{2,0,1:T(4,128)S(1)} %constant_dynamic-update-slice_fusion.4) | copy-start | bytes 92164
  342.9 68.8 %copy-start.1 = (s32[3,2560]{1,0:T(4,128)S(1)}, s32[3,2560]{1,0:T(4,128)}, u32[]{:S(2)}) copy-start(s32[3,2560]{1,0:T(4,128)} %param.23) | copy-start | bytes 92164
Sparse Core Ops, SparseCore 0:
  64.4 197.0 all-gather.1
